TPU v7x, 128 devices: a whole 4x4x4 slice. The times are simulated.
128 devices in a mesh: box: 32 (over y, z, core), tx: 4 (over x).
Axes of the slice: x: 4, y: 4, z: 4, core: 2. Of those that a mesh axis runs over, the one named last changes fastest.
Arguments:
- bank: bfloat16 [512, 1024, 1024], P('box', 'tx'), may hold values from -6 to 6
- pick: int32 [64], replicated, may hold values from 0 to 1023, as said below
- slot_box: int32 [512], replicated, may hold values from 0 to 511, each once
- leaf_factor: bfloat16 [512, 512, 128], P('box'), may hold values from -0.1875 to 0.1875
- self_factor: bfloat16 [9, 512, 64, 128], P(None, 'box'), may hold values from -0.375 to 0.375
- cross_factor: bfloat16 [9, 512, 64, 128], P(None, 'box'), may hold values from -0.375 to 0.375
- target_factor: bfloat16 [512, 64, 4096], P('box'), may hold values from -0.5 to 0.5
Outputs:
- field: bfloat16 [512, 64, 4096], P('box', 'tx')
Inputs may be any that keep to these rules, and one draw needn't show every extreme that they name: `pick`: distinct stored transmitters. `slot_box`: each box once.
All inputs are finite; a program needn't handle non-finite values.
Results may differ from a plain program's by a relative error of at most 0.023.
Values may be sent and summed in bfloat16 or wider, within the bound.
A program may use at most 128 MiB of HBM per device.

v0:
```python
import jax
import jax.numpy as jnp
from jax import lax
from jax.sharding import PartitionSpec as P


def partner_2(block, axis, bit):
    count = lax.axis_size(axis)
    route = []
    for low in range(count):
        high = low | 1 << bit
        if high != low and high < count:
            route += [(low, high), (high, low)]
    return lax.ppermute(block, axis, route)


def complex_times(values, matrix):
    inner = matrix.shape[-2]
    half = matrix.shape[-1] // 2
    first = jnp.einsum(
        "brn,bnk->brk", values[..., :inner], matrix, preferred_element_type=jnp.float32
    )
    second = jnp.einsum(
        "brn,bnk->brk", values[..., inner:], matrix, preferred_element_type=jnp.float32
    )
    return jnp.concatenate(
        [first[..., :half] - second[..., half:], first[..., half:] + second[..., :half]], axis=-1
    )


def per_device(bank, pick, slot_box, leaf_factor, self_factor, cross_factor, target_factor):
    box_dev = bank.shape[0]
    bank_dev = bank.shape[1]
    tx_index = lax.axis_index("tx")
    local_pick = pick - tx_index * bank_dev
    chooser = (local_pick[:, None] == jnp.arange(bank_dev, dtype=jnp.int32)[None, :]).astype(
        jnp.bfloat16
    )
    picked = jnp.einsum("pj,bju->bpu", chooser, bank, preferred_element_type=jnp.float32)
    owned = lax.psum_scatter(picked.astype(jnp.bfloat16), "tx", scatter_dimension=1, tiled=True)
    coefs = complex_times(owned, leaf_factor).astype(jnp.bfloat16)
    box_index = lax.axis_index("box")
    sources = lax.dynamic_slice_in_dim(slot_box, box_index * box_dev, box_dev)
    piece = lax.all_gather(coefs, "box", axis=0, tiled=True)
    count = piece.shape[0]
    taker = (sources[:, None] == jnp.arange(count, dtype=jnp.int32)[None, :]).astype(jnp.bfloat16)
    current = jnp.einsum("sn,nrk->srk", taker, piece, preferred_element_type=jnp.float32).astype(
        jnp.bfloat16
    )
    levels = self_factor.shape[0]
    local_bits = box_dev.bit_length() - 1
    for level in range(levels):
        if level < local_bits:
            span = 1 << level
            shaped = current.reshape(
                box_dev // (2 * span), 2, span, current.shape[1], current.shape[2]
            )
            partner = jnp.flip(shaped, axis=1).reshape(current.shape)
        else:
            partner = partner_2(current, "box", level - local_bits)
        mixed = complex_times(current, self_factor[level]) + complex_times(
            partner, cross_factor[level]
        )
        current = mixed.astype(jnp.bfloat16)
    return complex_times(current, target_factor).astype(jnp.bfloat16)


def solution(mesh):
    in_specs = (
        P("box", "tx", None),
        P(),
        P(),
        P("box", None, None),
        P(None, "box", None, None),
        P(None, "box", None, None),
        P("box", None, None),
    )
    out_specs = P("box", "tx", None)
    return jax.shard_map(
        per_device, mesh=mesh, in_specs=in_specs, out_specs=out_specs, check_vma=False
    )
```

profile of v0, /device:TPU:0, one launch (start us, length us, event | category | flops | bytes accessed | tf_op | source)
XLA Modules:
  0.0 153.6 jit_solution(15288603705547300182)
XLA Ops:
  7.3 6.3 %convert_bitcast_fusion = bf16[16,64,1024]{2,1,0:T(8,128)(2,1)} fusion(bf16[16,256,1024]{2,1,0:T(8,128)(2,1)} %param.7, s32[64]{0:T(128)S(1)} %broadcast_subtract_fusion), kind=kOutput, calls=%fused_computation.7 | convolution fusion | flops 537935872 | bytes 10486016 | tf_op jit(solution)/shard_map/pj,bju->bpu/dot_general | solution.py:39
  13.8 32.2 %reduce-scatter.2.cloned.1.call-done = bf16[16,16,1024]{2,1,0:T(8,128)(2,1)} async-done(((bf16[16,64,1024]{2,1,0:T(8,128)(2,1)}), bf16[16,16,1024]{2,1,0:T(8,128)(2,1)}) %reduce-scatter.2.cloned.1.call-update) | async-done | bytes 524304 | tf_op jit(solution)/shard_map/reduce_scatter | solution.py:40
  46.0 1.4 fusion.7
  49.4 43.1 %all-gather.2.cloned.1.call-done = bf16[512,16,128]{2,1,0:T(8,128)(2,1)} async-done(((bf16[16,16,128]{2,1,0:T(8,128)(2,1)}), bf16[512,16,128]{2,1,0:T(8,128)(2,1)}) %all-gather.2.cloned.1.call-update) | async-done | bytes 2097168 | tf_op jit(solution)/shard_map/all_gather | solution.py:44
  92.6 2.0 %fusion.4 = bf16[16,16,128]{2,0,1:T(8,128)(2,1)S(1)} fusion(bf16[512,16,128]{2,1,0:T(8,128)(2,1)} %all-gather.2.cloned.1.call-done, s32[16]{0:T(128)S(1)} %dynamic_slice.3), kind=kOutput, calls=%fused_computation.8 | convolution fusion | flops 33595392 | bytes 2162752 | tf_op jit(solution)/shard_map/sn,nrk->srk/dot_general | solution.py:47
  94.9 1.2 fusion.75
  96.1 1.1 fusion.77
  97.4 1.1 fusion.81
  98.5 1.1 fusion.79
  100.1 1.2 fusion.67
  101.3 1.1 fusion.69
  102.5 1.2 fusion.71
  103.7 1.1 fusion.73
  105.4 1.2 fusion.59
  106.6 1.1 fusion.61
  107.7 1.2 fusion.63
  109.0 1.1 fusion.65
  110.7 1.3 fusion.51
  112.1 1.1 fusion.53
  113.2 1.4 fusion.55
  114.6 1.1 fusion.57
  118.2 1.3 collective-permute-start.1
  120.0 2.5 %collective-permute-done.1 = bf16[16,16,128]{2,1,0:T(8,128)(2,1)S(1)} collective-permute-done((bf16[16,16,128]{2,1,0:T(8,128)(2,1)S(1)}, bf16[16,16,128]{2,1,0:T(8,128)(2,1)S(1)}, u32[]{:S(2)}, u32[]{:S(2)}) %collective-permute-start.1) | collective-permute-done | bytes 65568 | tf_op jit(solution)/shard_map/ppermute | solution.py:14
  123.3 2.4 %collective-permute-start.2 = (bf16[16,16,128]{2,1,0:T(8,128)(2,1)S(1)}, bf16[16,16,128]{2,1,0:T(8,128)(2,1)S(1)}, u32[]{:S(2)}, u32[]{:S(2)}) collective-permute-start(bf16[16,16,128]{2,1,0:T(8,128)(2,1)S(1)} %fusion.129), channel_id=1, source_target_pairs={{0,16},{16,0},{4,20},{20,4},{8,24},{24,8},{12,28},{28,12},{32,48},... | collective-permute-start | bytes 196616 | tf_op jit(solution)/shard_map/ppermute | solution.py:14
  126.2 2.9 %collective-permute-done.2 = bf16[16,16,128]{2,1,0:T(8,128)(2,1)S(1)} collective-permute-done((bf16[16,16,128]{2,1,0:T(8,128)(2,1)S(1)}, bf16[16,16,128]{2,1,0:T(8,128)(2,1)S(1)}, u32[]{:S(2)}, u32[]{:S(2)}) %collective-permute-start.2) | collective-permute-done | bytes 65568 | tf_op jit(solution)/shard_map/ppermute | solution.py:14
  129.9 1.3 collective-permute-start.3
  131.7 2.5 %collective-permute-done.3 = bf16[16,16,128]{2,1,0:T(8,128)(2,1)S(1)} collective-permute-done((bf16[16,16,128]{2,1,0:T(8,128)(2,1)S(1)}, bf16[16,16,128]{2,1,0:T(8,128)(2,1)S(1)}, u32[]{:S(2)}, u32[]{:S(2)}) %collective-permute-start.3) | collective-permute-done | bytes 65568 | tf_op jit(solution)/shard_map/ppermute | solution.py:14
  134.9 2.7 %collective-permute-start.4 = (bf16[16,16,128]{2,1,0:T(8,128)(2,1)S(1)}, bf16[16,16,128]{2,1,0:T(8,128)(2,1)S(1)}, u32[]{:S(2)}, u32[]{:S(2)}) collective-permute-start(bf16[16,16,128]{2,1,0:T(8,128)(2,1)S(1)} %fusion.131), channel_id=1, source_target_pairs={{0,64},{64,0},{4,68},{68,4},{8,72},{72,8},{12,76},{76,12},{16,80},... | collective-permute-start | bytes 196616 | tf_op jit(solution)/shard_map/ppermute | solution.py:14
  138.2 2.8 %collective-permute-done.4 = bf16[16,16,128]{2,1,0:T(8,128)(2,1)S(1)} collective-permute-done((bf16[16,16,128]{2,1,0:T(8,128)(2,1)S(1)}, bf16[16,16,128]{2,1,0:T(8,128)(2,1)S(1)}, u32[]{:S(2)}, u32[]{:S(2)}) %collective-permute-start.4) | collective-permute-done | bytes 65568 | tf_op jit(solution)/shard_map/ppermute | solution.py:14
  141.7 1.3 fusion.133
  143.0 1.2 fusion.135
  145.3 1.5 pad_maximum_fusion
  (80 shorter events, 13.6 us)
Async XLA Ops:
  6.5 39.4 %copy-start = (bf16[16,512,128]{2,1,0:T(8,128)(2,1)S(1)}, bf16[16,512,128]{2,1,0:T(8,128)(2,1)}, u32[]{:S(2)}) copy-start(bf16[16,512,128]{2,1,0:T(8,128)(2,1)} %param.10) | copy-start | bytes 6291460
  6.5 39.4 %reduce-scatter.2.cloned.1.call-start = ((), (), s32[]{:S(2)}) async-start(), calls=%async_computation.1 | async-start | bytes 2621440 | tf_op jit(solution)/shard_map/reduce_scatter | solution.py:40
  13.7 78.9 %all-gather.2.cloned.1.call-start = ((), (), s32[]{:S(2)}) async-start(), calls=%async_computation.2 | async-start | bytes 2162688 | tf_op jit(solution)/shard_map/all_gather | solution.py:44
  46.0 1.4 copy-start.3
  110.7 5.8 %copy-start.1 = (bf16[9,16,64,128]{3,2,1,0:T(8,128)(2,1)S(1)}, bf16[9,16,64,128]{3,2,1,0:T(8,128)(2,1)}, u32[]{:S(2)}) copy-start(bf16[9,16,64,128]{3,2,1,0:T(8,128)(2,1)} %param.11) | copy-start | bytes 7077892
  113.2 4.3 %copy-start.2 = (bf16[9,16,64,128]{3,2,1,0:T(8,128)(2,1)S(1)}, bf16[9,16,64,128]{3,2,1,0:T(8,128)(2,1)}, u32[]{:S(2)}) copy-start(bf16[9,16,64,128]{3,2,1,0:T(8,128)(2,1)} %param.12) | copy-start | bytes 7077892
  116.1 1.3 collective-permute-start
  118.2 4.3 %collective-permute-start.1 = (bf16[16,16,128]{2,1,0:T(8,128)(2,1)S(1)}, bf16[16,16,128]{2,1,0:T(8,128)(2,1)S(1)}, u32[]{:S(2)}, u32[]{:S(2)}) collective-permute-start(bf16[16,16,128]{2,1,0:T(8,128)(2,1)S(1)} %fusion.128), channel_id=1, source_target_pairs={{0,8},{8,0},{4,12},{12,4},{16,24},{24,16},{20,28},{28,20},{32,40},... | collective-permute-start | bytes 196616 | tf_op jit(solution)/shard_map/ppermute | solution.py:14
  119.9 21.8 %slice-start = ((s8[8388608]{0:T(1024)(128)(4,1)}), s8[4194304]{0:T(1024)(128)(4,1)S(1)}, s32[]{:S(2)}) async-start(s8[8388608]{0:T(1024)(128)(4,1)} %bitcast.120), calls=%async_computation.3 | async-start | bytes 8388608
  123.3 5.8 %collective-permute-start.2 = (bf16[16,16,128]{2,1,0:T(8,128)(2,1)S(1)}, bf16[16,16,128]{2,1,0:T(8,128)(2,1)S(1)}, u32[]{:S(2)}, u32[]{:S(2)}) collective-permute-start(bf16[16,16,128]{2,1,0:T(8,128)(2,1)S(1)} %fusion.129), channel_id=1, source_target_pairs={{0,16},{16,0},{4,20},{20,4},{8,24},{24,8},{12,28},{28,12},{32,48},... | collective-permute-start | bytes 196616 | tf_op jit(solution)/shard_map/ppermute | solution.py:14
  129.8 11.9 %slice-start.1 = ((s8[8388608]{0:T(1024)(128)(4,1)}), s8[4194304]{0:T(1024)(128)(4,1)S(1)}, s32[]{:S(2)}) async-start(s8[8388608]{0:T(1024)(128)(4,1)} %bitcast.120), calls=%async_computation.4 | async-start | bytes 8388608
  129.9 4.3 %collective-permute-start.3 = (bf16[16,16,128]{2,1,0:T(8,128)(2,1)S(1)}, bf16[16,16,128]{2,1,0:T(8,128)(2,1)S(1)}, u32[]{:S(2)}, u32[]{:S(2)}) collective-permute-start(bf16[16,16,128]{2,1,0:T(8,128)(2,1)S(1)} %fusion.130), channel_id=1, source_target_pairs={{0,32},{32,0},{4,36},{36,4},{8,40},{40,8},{12,44},{44,12},{16,48},... | collective-permute-start | bytes 196616 | tf_op jit(solution)/shard_map/ppermute | solution.py:14
  134.9 6.0 %collective-permute-start.4 = (bf16[16,16,128]{2,1,0:T(8,128)(2,1)S(1)}, bf16[16,16,128]{2,1,0:T(8,128)(2,1)S(1)}, u32[]{:S(2)}, u32[]{:S(2)}) collective-permute-start(bf16[16,16,128]{2,1,0:T(8,128)(2,1)S(1)} %fusion.131), channel_id=1, source_target_pairs={{0,64},{64,0},{4,68},{68,4},{8,72},{72,8},{12,76},{76,12},{16,80},... | collective-permute-start | bytes 196616 | tf_op jit(solution)/shard_map/ppermute | solution.py:14
Sparse Core Ops, SparseCore 0:
  13.8 32.0 reduce-scatter.1
  48.8 43.7 all-gather.1
where the time goes:
time: 154 us
  waiting for transfers between devices  86.4 us (56%)
  matrix products  35.8 us (23%)
  between operations  13.9 us (9%)
  other arithmetic  8.3 us (5%)
  starting transfers between devices  7.97 us (5%)
    all_gather x1, waiting for transfers between devices, per_device(): piece = lax.all_gather(coefs, 'box', axis=0, tiled=True)  43.1 us
    reduce_scatter x1, waiting for transfers between devices, per_device(): lax.psum_scatter(picked.astype(jnp.bfloat16), 'tx', scatter_dimension=1,...  32.2 us
    dot_general x20, matrix products, complex_times(): jnp.einsum('brn,bnk->brk', values[..., inner:], matrix, preferred_element...  15 us
    dot_general x20, matrix products, complex_times(): jnp.einsum('brn,bnk->brk', values[..., :inner], matrix, preferred_element...  12.5 us
    ppermute x5, waiting for transfers between devices, partner_2(): return lax.ppermute(block, axis, route)  11 us
    ppermute x5, starting transfers between devices, partner_2(): return lax.ppermute(block, axis, route)  7.93 us
    dot_general x1, matrix products, per_device(): jnp.einsum('pj,bju->bpu', chooser, bank, preferred_element_type=jnp.float32)  6.33 us
  transfers between devices with their start and end apart: 7, of which 7 were waited for; matrix products, arithmetic and copies ran while one was open for 2% of the time, Pallas kernels for 0%

commit v1 on v0

--- a/solution.py
+++ b/solution.py
@@ -41,7 +41,9 @@
     coefs = complex_times(owned, leaf_factor).astype(jnp.bfloat16)
     box_index = lax.axis_index("box")
     sources = lax.dynamic_slice_in_dim(slot_box, box_index * box_dev, box_dev)
-    piece = lax.all_gather(coefs, "box", axis=0, tiled=True)
+    piece = jnp.concatenate(
+        lax.all_to_all(jnp.stack([coefs] * lax.axis_size("box")), "box", 0, 0), axis=0
+    )
     count = piece.shape[0]
     taker = (sources[:, None] == jnp.arange(count, dtype=jnp.int32)[None, :]).astype(jnp.bfloat16)
     current = jnp.einsum("sn,nrk->srk", taker, piece, preferred_element_type=jnp.float32).astype(

time: 154 us -> 149 us (0.968)
  waiting for transfers between devices: 86.4 us -> 78.2 us
  local copies, waits for them, and re-layouts: 1.22 us -> 5.17 us
  matrix products: 35.8 us -> 34.2 us
    all_gather x1 -> x0, waiting for transfers between devices: 43.1 us -> none  [per_device(): piece = lax.all_gather(coefs, 'box', axis=0, tiled=True)]
    all_to_all x0 -> x1, waiting for transfers between devices: none -> 28.1 us  [per_device(): lax.all_to_all(jnp.stack([coefs] * lax.axis_size('box')), 'box', 0, 0)]
    all_to_all x0 -> x1, starting transfers between devices: none -> 7.4 us  [per_device(): lax.all_to_all(jnp.stack([coefs] * lax.axis_size('box')), 'box', 0, 0)]
    ppermute x5, waiting for transfers between devices: 11 us -> 17.8 us  [partner_2(): return lax.ppermute(block, axis, route)]
    ppermute x5, starting transfers between devices: 7.93 us -> 1.57 us  [partner_2(): return lax.ppermute(block, axis, route)]
    all_to_all x0 -> x1, local copies, waits for them, and re-layouts: none -> 2.13 us  [per_device(): lax.all_to_all(jnp.stack([coefs] * lax.axis_size('box')), 'box', 0, 0)]
    another operation x0 -> x1, local copies, waits for them, and re-layouts: none -> 1.79 us  [per_device(): jnp.stack([coefs] * lax.axis_size('box'))]
    dot_general x1, matrix products: 2.02 us -> 0.42 us  [per_device(): jnp.einsum('sn,nrk->srk', taker, piece, preferred_element_type=jnp.float32)]
where the time goes in v1:
time: 149 us; the launch traced here: 148 us
  waiting for transfers between devices  78.2 us (52%)
  matrix products  34.2 us (23%)
  between operations  13.9 us (9%)
  starting transfers between devices  8.98 us (6%)
  other arithmetic  7.67 us (5%)
  local copies, waits for them, and re-layouts  5.17 us (3%)
    reduce_scatter x1, waiting for transfers between devices, per_device(): lax.psum_scatter(picked.astype(jnp.bfloat16), 'tx', scatter_dimension=1,...  32.2 us
    all_to_all x1, waiting for transfers between devices, per_device(): lax.all_to_all(jnp.stack([coefs] * lax.axis_size('box')), 'box', 0, 0)  28.1 us
    ppermute x5, waiting for transfers between devices, partner_2(): return lax.ppermute(block, axis, route)  17.8 us
    dot_general x20, matrix products, complex_times(): jnp.einsum('brn,bnk->brk', values[..., inner:], matrix, preferred_element...  15 us
    dot_general x20, matrix products, complex_times(): jnp.einsum('brn,bnk->brk', values[..., :inner], matrix, preferred_element...  12.5 us
    all_to_all x1, starting transfers between devices, per_device(): lax.all_to_all(jnp.stack([coefs] * lax.axis_size('box')), 'box', 0, 0)  7.4 us
    dot_general x1, matrix products, per_device(): jnp.einsum('pj,bju->bpu', chooser, bank, preferred_element_type=jnp.float32)  6.33 us
  transfers between devices with their start and end apart: 7, of which 7 were waited for; matrix products, arithmetic and copies ran while one was open for 2% of the time, Pallas kernels for 0%

profile of v1, /device:TPU:0, one launch (start us, length us, event | category | flops | bytes accessed | tf_op | source)
XLA Modules:
  0.0 148.1 jit_solution(6392007470722562417)
XLA Ops:
  7.3 6.3 %convert_bitcast_fusion = bf16[16,64,1024]{2,1,0:T(8,128)(2,1)} fusion(bf16[16,256,1024]{2,1,0:T(8,128)(2,1)} %param.7, s32[64]{0:T(128)S(1)} %broadcast_subtract_fusion), kind=kOutput, calls=%fused_computation.5 | convolution fusion | flops 537935872 | bytes 10486016 | tf_op jit(solution)/shard_map/pj,bju->bpu/dot_general | solution.py:39
  13.7 32.2 %reduce-scatter.2.cloned.1.call-done = bf16[16,16,1024]{2,1,0:T(8,128)(2,1)} async-done(((bf16[16,64,1024]{2,1,0:T(8,128)(2,1)}), bf16[16,16,1024]{2,1,0:T(8,128)(2,1)}) %reduce-scatter.2.cloned.1.call-update) | async-done | bytes 524304 | tf_op jit(solution)/shard_map/reduce_scatter | solution.py:40
  46.0 1.4 fusion.2
  48.0 1.8 %stack.2 = bf16[32,16,16,128]{3,1,2,0:T(8,128)(2,1)} broadcast(bf16[16,16,128]{2,0,1:T(8,128)(2,1)S(1)} %copy.12), dimensions={1,2,3} | broadcast | bytes 2162688 | tf_op jit(solution)/shard_map/stack | solution.py:45
  49.8 7.4 %all-to-all-start = ((bf16[32,16,16,128]{3,1,2,0:T(8,128)(2,1)}), bf16[32,16,16,128]{3,1,2,0:T(8,128)(2,1)}, u32[]{:S(2)}, u32[]{:S(2)}) async-start(bf16[32,16,16,128]{3,1,2,0:T(8,128)(2,1)} %stack.2), calls=%async_computation.1 | async-start | bytes 4194304 | tf_op jit(solution)/shard_map/all_to_all | solution.py:45
  58.0 28.1 %all-to-all-done = bf16[32,16,16,128]{3,1,2,0:T(8,128)(2,1)} async-done(((bf16[32,16,16,128]{3,1,2,0:T(8,128)(2,1)}), bf16[32,16,16,128]{3,1,2,0:T(8,128)(2,1)}, u32[]{:S(2)}, u32[]{:S(2)}) %all-to-all-start) | async-done | bytes 2097184 | tf_op jit(solution)/shard_map/all_to_all | solution.py:45
  86.1 2.1 %copy.13 = bf16[32,16,16,128]{3,1,0,2:T(8,128)(2,1)S(1)} copy(bf16[32,16,16,128]{3,1,2,0:T(8,128)(2,1)} %all-to-all-done) | data formatting | bytes 4194304 | tf_op jit(solution)/shard_map/all_to_all | solution.py:45
  89.0 1.2 fusion.70
  90.2 1.1 fusion.72
  91.5 1.1 fusion.76
  92.6 1.1 fusion.74
  94.3 1.2 fusion.62
  95.5 1.1 fusion.64
  96.6 1.2 fusion.66
  97.8 1.1 fusion.68
  99.5 1.2 fusion.54
  100.7 1.1 fusion.56
  101.9 1.2 fusion.58
  103.1 1.1 fusion.60
  104.8 1.3 fusion.46
  106.2 1.1 fusion.48
  107.3 1.4 fusion.50
  108.7 1.1 fusion.52
  113.0 3.7 %collective-permute-done.1 = bf16[16,16,128]{2,1,0:T(8,128)(2,1)S(1)} collective-permute-done((bf16[16,16,128]{2,1,0:T(8,128)(2,1)S(1)}, bf16[16,16,128]{2,1,0:T(8,128)(2,1)S(1)}, u32[]{:S(2)}, u32[]{:S(2)}) %collective-permute-start.1) | collective-permute-done | bytes 65568 | tf_op jit(solution)/shard_map/ppermute | solution.py:14
  117.4 1.0 collective-permute-start.2
  119.0 4.3 %collective-permute-done.2 = bf16[16,16,128]{2,1,0:T(8,128)(2,1)S(1)} collective-permute-done((bf16[16,16,128]{2,1,0:T(8,128)(2,1)S(1)}, bf16[16,16,128]{2,1,0:T(8,128)(2,1)S(1)}, u32[]{:S(2)}, u32[]{:S(2)}) %collective-permute-start.2) | collective-permute-done | bytes 65568 | tf_op jit(solution)/shard_map/ppermute | solution.py:14
  124.7 4.1 %collective-permute-done.3 = bf16[16,16,128]{2,1,0:T(8,128)(2,1)S(1)} collective-permute-done((bf16[16,16,128]{2,1,0:T(8,128)(2,1)S(1)}, bf16[16,16,128]{2,1,0:T(8,128)(2,1)S(1)}, u32[]{:S(2)}, u32[]{:S(2)}) %collective-permute-start.3) | collective-permute-done | bytes 65568 | tf_op jit(solution)/shard_map/ppermute | solution.py:14
  130.4 5.1 %collective-permute-done.4 = bf16[16,16,128]{2,1,0:T(8,128)(2,1)S(1)} collective-permute-done((bf16[16,16,128]{2,1,0:T(8,128)(2,1)S(1)}, bf16[16,16,128]{2,1,0:T(8,128)(2,1)S(1)}, u32[]{:S(2)}, u32[]{:S(2)}) %collective-permute-start.4) | collective-permute-done | bytes 65568 | tf_op jit(solution)/shard_map/ppermute | solution.py:14
  136.3 1.3 fusion.128
  137.5 1.2 fusion.130
  138.8 1.1 fusion.1
  139.8 1.5 pad_maximum_fusion
  (82 shorter events, 12.8 us)
Async XLA Ops:
  6.5 39.4 %copy-start = (bf16[16,512,128]{2,1,0:T(8,128)(2,1)S(1)}, bf16[16,512,128]{2,1,0:T(8,128)(2,1)}, u32[]{:S(2)}) copy-start(bf16[16,512,128]{2,1,0:T(8,128)(2,1)} %param.10) | copy-start | bytes 6291460
  6.5 39.4 %reduce-scatter.2.cloned.1.call-start = ((), (), s32[]{:S(2)}) async-start(), calls=%async_computation.2 | async-start | bytes 2621440 | tf_op jit(solution)/shard_map/reduce_scatter | solution.py:40
  46.0 1.4 copy-start.3
  49.8 36.3 %all-to-all-start = ((bf16[32,16,16,128]{3,1,2,0:T(8,128)(2,1)}), bf16[32,16,16,128]{3,1,2,0:T(8,128)(2,1)}, u32[]{:S(2)}, u32[]{:S(2)}) async-start(bf16[32,16,16,128]{3,1,2,0:T(8,128)(2,1)} %stack.2), calls=%async_computation.1 | async-start | bytes 4194304 | tf_op jit(solution)/shard_map/all_to_all | solution.py:45
  104.8 5.5 %copy-start.1 = (bf16[9,16,64,128]{3,2,1,0:T(8,128)(2,1)S(1)}, bf16[9,16,64,128]{3,2,1,0:T(8,128)(2,1)}, u32[]{:S(2)}) copy-start(bf16[9,16,64,128]{3,2,1,0:T(8,128)(2,1)} %param.11) | copy-start | bytes 7077892
  107.3 4.3 %copy-start.2 = (bf16[9,16,64,128]{3,2,1,0:T(8,128)(2,1)S(1)}, bf16[9,16,64,128]{3,2,1,0:T(8,128)(2,1)}, u32[]{:S(2)}) copy-start(bf16[9,16,64,128]{3,2,1,0:T(8,128)(2,1)} %param.12) | copy-start | bytes 7077892
  110.2 1.3 collective-permute-start
  112.3 4.3 %collective-permute-start.1 = (bf16[16,16,128]{2,1,0:T(8,128)(2,1)S(1)}, bf16[16,16,128]{2,1,0:T(8,128)(2,1)S(1)}, u32[]{:S(2)}, u32[]{:S(2)}) collective-permute-start(bf16[16,16,128]{2,1,0:T(8,128)(2,1)S(1)} %fusion.123), channel_id=1, source_target_pairs={{0,8},{8,0},{4,12},{12,4},{16,24},{24,16},{20,28},{28,20},{32,40},... | collective-permute-start | bytes 196616 | tf_op jit(solution)/shard_map/ppermute | solution.py:14
  112.8 23.4 %slice-start = ((s8[8388608]{0:T(1024)(128)(4,1)}), s8[4194304]{0:T(1024)(128)(4,1)S(1)}, s32[]{:S(2)}) async-start(s8[8388608]{0:T(1024)(128)(4,1)} %bitcast.122), calls=%async_computation.3 | async-start | bytes 8388608
  117.4 5.8 %collective-permute-start.2 = (bf16[16,16,128]{2,1,0:T(8,128)(2,1)S(1)}, bf16[16,16,128]{2,1,0:T(8,128)(2,1)S(1)}, u32[]{:S(2)}, u32[]{:S(2)}) collective-permute-start(bf16[16,16,128]{2,1,0:T(8,128)(2,1)S(1)} %fusion.124), channel_id=1, source_target_pairs={{0,16},{16,0},{4,20},{20,4},{8,24},{24,8},{12,28},{28,12},{32,48},... | collective-permute-start | bytes 196616 | tf_op jit(solution)/shard_map/ppermute | solution.py:14
  124.0 12.3 %slice-start.1 = ((s8[8388608]{0:T(1024)(128)(4,1)}), s8[4194304]{0:T(1024)(128)(4,1)S(1)}, s32[]{:S(2)}) async-start(s8[8388608]{0:T(1024)(128)(4,1)} %bitcast.122), calls=%async_computation.4 | async-start | bytes 8388608
  124.0 4.8 %collective-permute-start.3 = (bf16[16,16,128]{2,1,0:T(8,128)(2,1)S(1)}, bf16[16,16,128]{2,1,0:T(8,128)(2,1)S(1)}, u32[]{:S(2)}, u32[]{:S(2)}) collective-permute-start(bf16[16,16,128]{2,1,0:T(8,128)(2,1)S(1)} %fusion.125), channel_id=1, source_target_pairs={{0,32},{32,0},{4,36},{36,4},{8,40},{40,8},{12,44},{44,12},{16,48},... | collective-permute-start | bytes 196616 | tf_op jit(solution)/shard_map/ppermute | solution.py:14
  129.5 6.0 %collective-permute-start.4 = (bf16[16,16,128]{2,1,0:T(8,128)(2,1)S(1)}, bf16[16,16,128]{2,1,0:T(8,128)(2,1)S(1)}, u32[]{:S(2)}, u32[]{:S(2)}) collective-permute-start(bf16[16,16,128]{2,1,0:T(8,128)(2,1)S(1)} %fusion.126), channel_id=1, source_target_pairs={{0,64},{64,0},{4,68},{68,4},{8,72},{72,8},{12,76},{76,12},{16,80},... | collective-permute-start | bytes 196616 | tf_op jit(solution)/shard_map/ppermute | solution.py:14
Sparse Core Ops, SparseCore 0:
  13.8 32.0 reduce-scatter.1
